TPU v7x, 256 devices: a whole 4x4x8 slice. The times are simulated.
256 devices in a mesh: req: 16 (over y_hi, x, core), tp: 16 (over y_lo, z).
Axes of the slice: x: 4, y: 4 (y_hi: 2, y_lo: 2; y = y_hi * 2 + y_lo), z: 8, core: 2. Of those that a mesh axis runs over, the one named last changes fastest.
Arguments:
- tokens: bfloat16 [14336, 5120], P(('req', 'tp')), may hold values from -6 to 6
- qkv_weight: bfloat16 [5120, 3, 4096], P('req', None, 'tp')
- out_weight: bfloat16 [4096, 5120], P('tp', 'req')
- query_key_gain: float32 [2, 4096], P(None, 'tp'), may hold values from 0.25 to 1.75
- post_gain: float32 [5120], replicated, may hold values from 0.25 to 1.75
- pool_cache: bfloat16 [512, 128, 2, 4096], P('req', None, None, 'tp'), may hold values from -68 to 68
- lengths: int32 [16, 16], P('req'), may hold values from 1 to 256, 896 in all within a row
- prefix_pages: int32 [16, 16], P('req'), may hold values from 1 to 16, 32 in all within a row
- pool_order: int32 [16, 32], P('req'), may hold values from 0 to 31, each once within a row
- owners: int32 [16, 16], P('req'), may hold values from 0 to 15, each once within a row
Outputs:
- hidden: bfloat16 [14336, 5120], P(('req', 'tp'))
- handed_pages: bfloat16 [512, 128, 2, 4096], P('req', None, None, 'tp')
Inputs may be any that keep to these rules, and one draw needn't show every extreme that they name: `lengths`: each row sums to 896; the largest entry of every row is exactly 256. `prefix_pages`: each row sums to 32; the largest entry of every row is exactly 16. `pool_order`: each row names every slot once. `owners`: each row names every owner once.
All inputs are finite; a program needn't handle non-finite values.
Results may differ from a plain program's by a relative error of at most 0.014.
Values may be sent and summed in bfloat16 or wider, within the bound.
A program may use at most 128 MiB of HBM per device.

v0:
```python
import functools

import jax
import jax.numpy as jnp
from jax import lax
from jax.experimental import pallas as pl
from jax.experimental.pallas import tpu as pltpu
from jax.sharding import PartitionSpec as P

HEADS = 32
HEAD = 128
PAGE = 128
CAP = 2
QTILE = 128
CHUNK = 512

norm_eps = 1e-06
rope_base = 500000.0
masked_score = -1e30
log2_e = 1.4426950408889634
MESH = pl.DeviceIdType.MESH


def token_layout(lengths_row, prefix_row, block_len):
    ends_at = jnp.cumsum(lengths_row)
    starts_at = ends_at - lengths_row
    token_ids = jnp.arange(block_len, dtype=jnp.int32)
    request_of = jnp.sum((token_ids[:, None] >= ends_at[None, :]).astype(jnp.int32), axis=1)
    one_hot = (
        request_of[:, None] == jnp.arange(lengths_row.shape[0], dtype=jnp.int32)[None, :]
    ).astype(jnp.int32)
    shift_of = jnp.sum(one_hot * (prefix_row * PAGE - starts_at)[None, :], axis=1)
    return (request_of, token_ids + shift_of, starts_at)


def rotate_heads(tensor, cosine, sine_part):
    half_dim = HEAD // 2
    first_half = tensor[..., :half_dim]
    second_half = tensor[..., half_dim:]
    return jnp.concatenate(
        [
            first_half * cosine - second_half * sine_part,
            second_half * cosine + first_half * sine_part,
        ],
        axis=-1,
    )


def sum_kernel(count, x_ref, o_ref, slots, send_sem, recv_sem):
    me = lax.axis_index("tp")
    barrier = pltpu.get_barrier_semaphore()
    for d in range(1, count):
        pl.semaphore_signal(
            barrier, inc=1, device_id={"tp": lax.rem(me + d, count)}, device_id_type=MESH
        )
    pl.semaphore_wait(barrier, count - 1)
    copies = []
    for d in range(1, count):
        copy = pltpu.make_async_remote_copy(
            src_ref=x_ref,
            dst_ref=slots.at[d - 1],
            send_sem=send_sem.at[d - 1],
            recv_sem=recv_sem.at[d - 1],
            device_id={"tp": lax.rem(me + d, count)},
            device_id_type=MESH,
        )
        copy.start()
        copies.append(copy)
    for copy in copies:
        copy.wait()
    total = x_ref[...]
    for d in range(1, count):
        total = total + slots[d - 1]
    o_ref[...] = total


def sum_over_tp(x, count):
    return pl.pallas_call(
        functools.partial(sum_kernel, count),
        out_shape=jax.ShapeDtypeStruct(x.shape, x.dtype),
        in_specs=[pl.BlockSpec(memory_space=pltpu.VMEM)],
        out_specs=pl.BlockSpec(memory_space=pltpu.VMEM),
        scratch_shapes=[
            pltpu.VMEM((count - 1,) + x.shape, x.dtype),
            pltpu.SemaphoreType.DMA((count - 1,)),
            pltpu.SemaphoreType.DMA((count - 1,)),
        ],
        compiler_params=pltpu.CompilerParams(collective_id=0, has_side_effects=True),
        cost_estimate=pl.CostEstimate(flops=100000, bytes_accessed=20000000, transcendentals=0),
        name="sum_squares",
    )(x)


def attend_kernel(
    bounds_ref, q_ref, kn_ref, vn_ref, kt_ref, vp_ref, row_ref, col_ref, key_ref, o_ref
):
    block_len, width = q_ref.shape
    heads_here = width // HEAD
    scale = HEAD ** (-0.5) * log2_e
    window = CAP * PAGE + QTILE

    def tile(i, _):
        r0 = pl.multiple_of(i * QTILE, QTILE)
        k0 = pl.multiple_of(jnp.maximum(i - CAP, 0) * QTILE, QTILE)
        tile_rows, tile_keys = pl.ds(r0, QTILE), pl.ds(k0, window)
        row_req = row_ref[tile_rows, :]
        row_ids = lax.broadcasted_iota(jnp.int32, (QTILE, window), 0) + r0
        col_ids = lax.broadcasted_iota(jnp.int32, (QTILE, window), 1) + k0
        block_mask = (row_req == col_ref[:, tile_keys]) & (col_ids <= row_ids)
        carry = []
        for h in range(heads_here):
            cols = slice(h * HEAD, (h + 1) * HEAD)
            scores = lax.dot_general(
                q_ref[tile_rows, cols],
                kn_ref[tile_keys, cols],
                (((1,), (1,)), ((), ())),
                preferred_element_type=jnp.float32,
            )
            scores = jnp.where(block_mask, scores * scale, masked_score)
            top = jnp.max(scores, axis=1, keepdims=True)
            weights = jnp.exp2(scores - top)
            total = jnp.sum(weights, axis=1, keepdims=True)
            mixed = jnp.dot(
                weights.astype(jnp.bfloat16), vn_ref[tile_keys, cols], preferred_element_type=jnp.float32
            )
            carry += [top, total, mixed]

        def step(j, carry):
            off = pl.multiple_of(j * CHUNK, CHUNK)
            mask = row_req == key_ref[:, pl.ds(off, CHUNK)]
            out = []
            for h in range(heads_here):
                cols = slice(h * HEAD, (h + 1) * HEAD)
                top, total, mixed = carry[3 * h : 3 * h + 3]
                scores = jnp.dot(
                    q_ref[tile_rows, cols],
                    kt_ref[cols, pl.ds(off, CHUNK)],
                    preferred_element_type=jnp.float32,
                )
                scores = jnp.where(mask, scores * scale, masked_score)
                new_top = jnp.maximum(top, jnp.max(scores, axis=1, keepdims=True))
                fade = jnp.exp2(top - new_top)
                weights = jnp.exp2(scores - new_top)
                total = total * fade + jnp.sum(weights, axis=1, keepdims=True)
                mixed = mixed * fade + jnp.dot(
                    weights.astype(jnp.bfloat16),
                    vp_ref[pl.ds(off, CHUNK), cols],
                    preferred_element_type=jnp.float32,
                )
                out += [new_top, total, mixed]
            return tuple(out)

        carry = lax.fori_loop(bounds_ref[0, i], bounds_ref[1, i], step, tuple(carry))
        for h in range(heads_here):
            cols = slice(h * HEAD, (h + 1) * HEAD)
            o_ref[tile_rows, cols] = (carry[3 * h + 2] / carry[3 * h + 1]).astype(jnp.bfloat16)
        return 0

    lax.fori_loop(0, block_len // QTILE, tile, 0)


def attend(bounds, q, kn, vn, kt, vp, row_req, col_req, key_req):
    vmem = pl.BlockSpec(memory_space=pltpu.VMEM)
    return pl.pallas_call(
        attend_kernel,
        out_shape=jax.ShapeDtypeStruct(q.shape, jnp.bfloat16),
        in_specs=[pl.BlockSpec(memory_space=pltpu.SMEM)] + [vmem] * 8,
        out_specs=vmem,
        cost_estimate=pl.CostEstimate(
            flops=4000000000, bytes_accessed=40000000, transcendentals=4000000
        ),
        name="paged_attention",
    )(bounds, q, kn, vn, kt, vp, row_req, col_req, key_req)


def gather_kernel(
    n_z, n_x, tok_ref, wq_ref, wo_ref, toks, wqs, wos, send_sem, recv_sem, local_sem
):
    tp, req = lax.axis_index("tp"), lax.axis_index("req")
    y, z = tp // n_z, lax.rem(tp, n_z)
    high, x, core = req // (2 * n_x), lax.rem(req // 2, n_x), lax.rem(req, 2)

    def token_slot(yy, dz):
        return yy * n_z + lax.rem(z + dz + n_z, n_z)

    def weight_slot(hh, dx, cc):
        return (hh * n_x + lax.rem(x + dx + n_x, n_x)) * 2 + cc

    up, down, across = (
        {"tp": token_slot(y, 1), "req": req},
        {"tp": token_slot(y, -1), "req": req},
        {"tp": token_slot(1 - y, 0), "req": req},
    )
    far, right, left, twin = (
        {"tp": tp, "req": weight_slot(1 - high, 0, core)},
        {"tp": tp, "req": weight_slot(high, 1, core)},
        {"tp": tp, "req": weight_slot(high, -1, core)},
        {"tp": tp, "req": weight_slot(high, 0, 1 - core)},
    )
    peers = (up, down, across, far, right, left, twin)

    barrier = pltpu.get_barrier_semaphore()
    for peer in peers:
        pl.semaphore_signal(barrier, inc=1, device_id=peer, device_id_type=MESH)
    pl.semaphore_wait(barrier, len(peers))

    copies = {}

    def push(name, src, dst, peer):
        index = len(copies)
        copies[name] = pltpu.make_async_remote_copy(
            src_ref=src,
            dst_ref=dst,
            send_sem=send_sem.at[index],
            recv_sem=recv_sem.at[index],
            device_id=peer,
            device_id_type=MESH,
        )
        copies[name].start()

    arrived = set()

    def await_one(name):
        copies[name].wait_recv()
        arrived.add(name)

    half = tok_ref.shape[1] // 2

    def send_token(name, part, slot, peer, own=False):
        cols = pl.ds(part * half, half)
        dst = toks.at[slot, :, cols]
        push((name, part), tok_ref.at[:, cols] if own else dst, dst, peer)

    rows = wq_ref.shape[0]

    def send_weight(name, slot, peer, own=False, part=None):
        span = pl.ds(0, rows) if part is None else pl.ds(part * (rows // 2), rows // 2)
        for tag, ref, out in (("q", wq_ref, wqs), ("o", wo_ref, wos)):
            dst = out.at[slot, span, :]
            push((name, tag), ref if own else dst, dst, peer)

    def await_weight(name):
        await_one((name, "q"))
        await_one((name, "o"))

    own_slot = token_slot(y, 0)
    own_weight = weight_slot(high, 0, core)
    for part in range(2):
        send_token("up0", part, own_slot, up, own=True)
        send_token("down0", part, own_slot, down, own=True)
        send_token("across0", part, own_slot, across, own=True)
    send_weight("right0", own_weight, right, own=True)
    send_weight("left0", own_weight, left, own=True)
    send_weight("far0", own_weight, far, own=True)
    send_weight("twin0", own_weight, twin, own=True)
    locals_ = [
        pltpu.make_async_copy(tok_ref, toks.at[own_slot], local_sem.at[0]),
        pltpu.make_async_copy(wq_ref, wqs.at[own_weight], local_sem.at[1]),
        pltpu.make_async_copy(wo_ref, wos.at[own_weight], local_sem.at[2]),
    ]
    for copy in locals_:
        copy.start()

    for part in range(2):
        await_one(("up0", part))
        send_token("up1", part, token_slot(y, -1), up)
        await_one(("down0", part))
        send_token("down1", part, token_slot(y, 1), down)
        await_one(("across0", part))
        send_token("pair_up0", part, token_slot(1 - y, 0), up)
        send_token("pair_down0", part, token_slot(1 - y, 0), down)

    await_weight("right0")
    send_weight("right1", weight_slot(high, -1, core), right, part=0)
    send_weight("twin1", weight_slot(high, -1, core), twin)
    await_weight("left0")
    send_weight("left1", weight_slot(high, 1, core), left, part=1)
    send_weight("twin2", weight_slot(high, 1, core), twin)
    await_weight("far0")
    send_weight("far_right0", weight_slot(1 - high, 0, core), right)
    send_weight("far_left0", weight_slot(1 - high, 0, core), left)
    send_weight("twin3", weight_slot(1 - high, 0, core), twin)

    for part in range(2):
        await_one(("up1", part))
        send_token("up2", part, token_slot(y, -2), up)
        send_token("across1", part, token_slot(y, -2), across)
        await_one(("down1", part))
        send_token("down2", part, token_slot(y, 2), down)
        await_one(("pair_down0", part))
        send_token("pair_down1", part, token_slot(1 - y, 1), down)

    await_weight("right1")
    await_weight("left1")
    send_weight("twin4", weight_slot(high, 2, core), twin)
    await_weight("far_right0")
    send_weight("far_right1", weight_slot(1 - high, -1, core), right, part=0)
    send_weight("twin5", weight_slot(1 - high, -1, core), twin)
    await_weight("far_left0")
    send_weight("far_left1", weight_slot(1 - high, 1, core), left, part=1)
    send_weight("twin6", weight_slot(1 - high, 1, core), twin)

    for part in range(2):
        await_one(("up2", part))
        send_token("up3", part, token_slot(y, -3), up)
        send_token("across2", part, token_slot(y, -3), across)
        await_one(("down2", part))
        send_token("across3", part, token_slot(y, 3), across)

    await_weight("far_right1")
    await_weight("far_left1")
    send_weight("twin7", weight_slot(1 - high, 2, core), twin)

    for part in range(2):
        await_one(("up3", part))
        send_token("across4", part, token_slot(y, -4), across)

    for name in copies:
        if name not in arrived:
            copies[name].wait_recv()
    for name in copies:
        copies[name].wait_send()
    for copy in locals_:
        copy.wait()


def gather_all(tokens, qkv_rows, out_rows, n_tp, n_req):
    vmem = pl.BlockSpec(memory_space=pltpu.VMEM)
    hbm = pl.BlockSpec(memory_space=pl.ANY)
    copies = 30 + 34
    return pl.pallas_call(
        functools.partial(gather_kernel, n_tp // 2, n_req // 4),
        out_shape=[
            jax.ShapeDtypeStruct((n_tp,) + tokens.shape, tokens.dtype),
            jax.ShapeDtypeStruct((n_req,) + qkv_rows.shape, qkv_rows.dtype),
            jax.ShapeDtypeStruct((n_req,) + out_rows.shape, out_rows.dtype),
        ],
        in_specs=[vmem] * 3,
        out_specs=[hbm] * 3,
        scratch_shapes=[
            pltpu.SemaphoreType.DMA((copies,)),
            pltpu.SemaphoreType.DMA((copies,)),
            pltpu.SemaphoreType.DMA((3,)),
        ],
        compiler_params=pltpu.CompilerParams(collective_id=1, has_side_effects=True),
        name="gather_all",
    )(tokens, qkv_rows, out_rows)


def body(
    tokens,
    qkv_weight,
    out_weight,
    query_key_gain,
    post_gain,
    pool_cache,
    lengths,
    prefix_pages,
    pool_order,
    owners,
):
    n_req = lax.axis_size("req")
    n_tp = lax.axis_size("tp")
    local_rows = qkv_weight.shape[0]
    local_width = qkv_weight.shape[2]
    qkv_width = 3 * local_width
    heads_here = local_width // HEAD
    block_tokens, qkv_full, out_full = gather_all(
        tokens, qkv_weight.reshape(local_rows, qkv_width), out_weight.T, n_tp, n_req
    )
    block_tokens = block_tokens.reshape(n_tp * tokens.shape[0], tokens.shape[1])
    qkv_full = qkv_full.reshape(n_req * local_rows, qkv_width)
    out_full = out_full.reshape(n_req * local_rows, local_width)
    block_len = block_tokens.shape[0]

    lengths_row = lengths[0]
    prefix_row = prefix_pages[0]
    order_row = pool_order[0]
    request_of, positions, starts_at = token_layout(lengths_row, prefix_row, block_len)
    half_dim = HEAD // 2
    frequency = rope_base ** (-(2.0 * jnp.arange(half_dim, dtype=jnp.float32)) / HEAD)
    angles = positions.astype(jnp.float32)[:, None] * frequency[None, :]
    cosine = jnp.cos(angles)[:, None, :]
    sine_part = jnp.sin(angles)[:, None, :]

    pool_count = pool_cache.shape[0]
    page_ends = jnp.cumsum(prefix_row)
    page_starts = page_ends - prefix_row
    page_ids = jnp.arange(pool_count, dtype=jnp.int32)
    page_request = jnp.sum((page_ids[:, None] >= page_ends[None, :]).astype(jnp.int32), axis=1)
    key_req = jnp.repeat(page_request, PAGE)[None, :]
    pool_keys = jnp.take(pool_cache[:, :, 0, :], order_row, axis=0)
    pool_values = jnp.take(pool_cache[:, :, 1, :], order_row, axis=0)
    keys_t = pool_keys.reshape(pool_count * PAGE, local_width).T
    pool_values = pool_values.reshape(pool_count * PAGE, local_width)
    tiles = block_len // QTILE
    first_req = request_of.reshape(tiles, QTILE)[:, 0]
    last_req = request_of.reshape(tiles, QTILE)[:, -1]
    req_ids = jnp.arange(lengths_row.shape[0], dtype=jnp.int32)
    low = jnp.sum(jnp.where(first_req[:, None] == req_ids[None, :], page_starts[None, :], 0), axis=1)
    high = jnp.sum(jnp.where(last_req[:, None] == req_ids[None, :], page_ends[None, :], 0), axis=1)
    per_chunk = CHUNK // PAGE
    bounds = jnp.stack([low // per_chunk, (high + per_chunk - 1) // per_chunk]).astype(jnp.int32)

    joined_all = jnp.dot(block_tokens, qkv_full, preferred_element_type=jnp.float32)
    queries = joined_all[:, :local_width]
    keys_raw = joined_all[:, local_width : 2 * local_width]
    values_raw = joined_all[:, 2 * local_width :]
    local_sums = jnp.stack(
        [jnp.sum(queries * queries, axis=1), jnp.sum(keys_raw * keys_raw, axis=1)]
    )
    global_sums = sum_over_tp(local_sums, n_tp)
    inverse = lax.rsqrt(global_sums / (HEADS * HEAD) + norm_eps)
    queries = queries * inverse[0][:, None] * query_key_gain[0]
    keys_raw = keys_raw * inverse[1][:, None] * query_key_gain[1]
    query_rot = (
        rotate_heads(queries.reshape(block_len, heads_here, HEAD), cosine, sine_part)
        .astype(jnp.bfloat16)
        .reshape(block_len, local_width)
    )
    key_rot = (
        rotate_heads(keys_raw.reshape(block_len, heads_here, HEAD), cosine, sine_part)
        .astype(jnp.bfloat16)
        .reshape(block_len, local_width)
    )
    value_new = values_raw.astype(jnp.bfloat16)

    page_span = CAP * PAGE
    owner_pick = (owners[0][None, :] == jnp.arange(n_req, dtype=jnp.int32)[:, None]).astype(jnp.int32)
    start_of = jnp.sum(owner_pick * starts_at[None, :], axis=1)
    length_of = jnp.sum(owner_pick * lengths_row[None, :], axis=1)
    offsets = jnp.arange(page_span, dtype=jnp.int32)
    source = jnp.where(
        offsets[None, :] < length_of[:, None], start_of[:, None] + offsets[None, :], -1
    ).reshape(-1)
    token_ids = jnp.arange(block_len, dtype=jnp.int32)
    select = (source[:, None] == token_ids[None, :]).astype(jnp.bfloat16)
    kv_new = jnp.concatenate([key_rot, value_new], axis=1)
    outgoing = jnp.dot(select, kv_new, preferred_element_type=jnp.float32).astype(jnp.bfloat16)
    arrived = lax.all_to_all(
        outgoing.reshape(n_req, page_span, 2 * local_width),
        "req",
        split_axis=0,
        concat_axis=0,
        tiled=True,
    )
    handed_pages = arrived.reshape(n_req * CAP, PAGE, 2, local_width)

    attention = attend(
        bounds,
        query_rot,
        key_rot,
        value_new,
        keys_t,
        pool_values,
        request_of[:, None],
        request_of[None, :],
        key_req,
    )
    partial = lax.dot_general(
        attention, out_full, (((1,), (1,)), ((), ())), preferred_element_type=jnp.float32
    ).astype(jnp.bfloat16)
    projected = lax.psum_scatter(partial, "tp", scatter_dimension=0, tiled=True).astype(jnp.float32)
    post_scale = lax.rsqrt(jnp.mean(projected * projected, axis=1, keepdims=True) + norm_eps)
    hidden = (tokens.astype(jnp.float32) + projected * post_scale * post_gain[None, :]).astype(
        jnp.bfloat16
    )
    return (hidden, handed_pages)


def solution(mesh):
    in_specs = (
        P(("req", "tp"), None),
        P("req", None, "tp"),
        P("tp", "req"),
        P(None, "tp"),
        P(),
        P("req", None, None, "tp"),
        P("req", None),
        P("req", None),
        P("req", None),
        P("req", None),
    )
    out_specs = (P(("req", "tp"), None), P("req", None, None, "tp"))
    return jax.shard_map(body, mesh=mesh, in_specs=in_specs, out_specs=out_specs, check_vma=False)
```

profile of v0, /device:TPU:1, one launch (start us, length us, event | category | flops | bytes accessed | tf_op | source)
XLA Modules:
  0.0 374.3 jit_solution(6444811243646612652)
XLA Ops:
  7.2 0.7 compare_select_fusion
  7.9 0.7 compare_and_fusion
  8.5 1.3 copy.49
  9.9 1.0 copy.50.wq_ref
  10.9 91.4 %gather_all.1 = (bf16[16,56,5120]{2,1,0:T(8,128)(2,1)}, bf16[16,320,768]{2,1,0:T(8,128)(2,1)}, bf16[16,320,256]{2,1,0:T(8,128)(2,1)}) custom-call(bf16[56,5120]{1,0:T(8,128)(2,1)} %tok_ref.1, bf16[320,768]{1,0:T(8,128)(2,1)} %copy.50.wq_ref, bf16[320,256]{1,0:T(8,128)(2,1)} %bitcast.87), custom_call_target="tpu_custom_call" | custom-call | tf_op jit(solution)/shard_map/gather_all/pallas_call | solution.py:331
  102.3 12.1 %fusion.17 = f32[896,768]{0,1:T(8,128)S(1)} fusion(bf16[896,5120]{1,0:T(8,128)(2,1)} %bitcast.97, bf16[5120,768]{1,0:T(8,128)(2,1)} %bitcast.98), kind=kOutput, calls=%fused_computation.82 | convolution fusion | flops 7046430720 | bytes 19791872 | tf_op jit(solution)/shard_map/dot_general | solution.py:405
  114.5 0.1 multiply_reduce_fusion.1
  114.7 0.4 copy-done.8
  115.2 0.1 reduce.2
  115.5 0.1 reduce
  115.8 0.9 broadcast_in_dim.84.row_ref
  116.8 0.6 pad_maximum_fusion.2.x_ref
  117.4 0.6 broadcast_in_dim.74.col_ref
  117.9 9.1 %sum_squares.1 = f32[2,896]{1,0:T(2,128)} custom-call(f32[2,896]{1,0:T(2,128)} %pad_maximum_fusion.2.x_ref), custom_call_target="tpu_custom_call" | custom-call | flops 100000 | bytes 20000000 | tf_op jit(solution)/shard_map/sum_squares/pallas_call | solution.py:78
  127.1 0.7 add_rsqrt_fusion
  127.8 1.1 multiply_multiply_fusion
  129.0 0.8 fusion.15
  129.8 0.9 copy.61
  130.7 1.8 copy.62
  132.5 1.0 fusion.14
  133.5 1.8 copy.63
  135.3 2.1 copy.64
  137.5 1.7 multiply_cosine_fusion
  139.2 3.0 subtract_convert_fusion
  142.2 2.5 pad_maximum_fusion
  144.7 0.9 copy.75
  145.6 0.8 copy.76
  146.4 0.2 slice_reduce_fusion.1
  146.6 0.2 select_reduce_fusion.3
  146.9 6.1 %fusion.13 = (bf16[32,128,1,256]{3,2,1,0:T(2,128)(2,1)S(1)}, bf16[32,128,1,256]{3,2,1,0:T(2,128)(2,1)S(1)}) fusion(bf16[32,128,2,256]{3,2,1,0:T(2,128)(2,1)S(1)} %copy-done), kind=kLoop, calls=%fused_computation.78 | loop fusion | bytes 8388608 | tf_op jit(solution)/shard_map/slice | solution.py:393
  153.0 3.2 copy_bitcast_fusion
  156.2 2.3 gather_fusion
  158.5 3.6 gather_fusion.1
  162.1 4.0 %broadcast_select_fusion = (bf16[32,128,256]{2,1,0:T(8,128)(2,1)}, bf16[32,128,256]{2,1,0:T(8,128)(2,1)}) fusion(bf16[32,128,256]{2,1,0:T(8,128)(2,1)} %gather_fusion.1, pred[32]{0:T(512)(128)(4,1)S(1)} %compare_and_fusion, bf16[32,128,256]{2,1,0:T(8,128)(2,1)S(1)} %gather_fusion), kind=kLoop, calls=%fused_computation.9 | loop fusion | flops 2097152 | bytes 8388640 | tf_op jit(solution)/shard_map/jit(_take)/select_n | solution.py:393
  166.1 4.1 %copy.60 = bf16[4096,256]{0,1:T(8,128)(2,1)} copy(bf16[4096,256]{1,0:T(8,128)(2,1)} %bitcast.74) | data formatting | bytes 4194304 | tf_op jit(solution)/shard_map/reshape | solution.py:394
  170.2 1.0 copy.67.vn_ref
  171.2 0.6 pad_add_fusion.bounds_ref
  171.8 0.7 broadcast_in_dim.75
  172.5 18.5 %paged_attention.1 = bf16[896,256]{1,0:T(8,128)(2,1)} custom-call(s32[2,7]{1,0:T(2,128)} %pad_add_fusion.bounds_ref, bf16[896,256]{1,0:T(8,128)(2,1)} %bitcast.86, bf16[896,256]{1,0:T(8,128)(2,1)} %bitcast.84, bf16[896,256]{1,0:T(8,128)(2,1)} %copy.67.vn_ref, bf16[256,4096]{1,0:T(8,128)(2,1)} %bitcast.80, bf16[4096,256]{1,0:T(8,128)(2,1)} %bitcast.81, ...), custom_call_target="tpu_custom_call" | custom-call | flops 4000000000 | bytes 40000000 | tf_op jit(solution)/shard_map/paged_attention/pallas_call | solution.py:164
  191.0 7.1 %convolution_convert_fusion = bf16[896,5120]{1,0:T(8,128)(2,1)} fusion(bf16[896,256]{1,0:T(8,128)(2,1)} %paged_attention.1, bf16[5120,256]{1,0:T(8,128)(2,1)S(1)} %bitcast.78), kind=kOutput, calls=%fused_computation.4 | convolution fusion | flops 2353397760 | bytes 12255232 | tf_op jit(solution)/shard_map/dot_general | solution.py:460
  198.2 0.6 copy-done.10
  199.0 0.2 copy-done.4
  199.2 0.1 copy-done.5
  199.3 4.8 %fusion.2 = bf16[4096,512]{1,0:T(8,128)(2,1)S(1)} fusion(s32[4096]{0:T(1024)S(1)} %bitcast.90, bf16[896,256]{1,0:T(8,128)(2,1)S(1)} %copy-done.5, bf16[896,256]{1,0:T(8,128)(2,1)S(1)} %bitcast.85), kind=kOutput, calls=%fused_computation.6 | convolution fusion | flops 3765698560 | bytes 5128192 | tf_op jit(solution)/shard_map/dot_general | solution.py:439
  204.1 152.9 %all_to_all.5 = bf16[16,256,512]{2,1,0:T(8,128)(2,1)} all-to-all(bf16[16,256,512]{2,1,0:T(8,128)(2,1)S(1)} %bitcast.75), channel_id=1, replica_groups=mesh['req'=16,'tp'=16] {'req'}, dimensions={0} | all-to-all | bytes 8388608 | tf_op jit(solution)/shard_map/all_to_all | solution.py:440
  357.0 6.9 %reshape.293 = bf16[32,128,2,256]{3,2,1,0:T(2,128)(2,1)} reshape(bf16[16,256,512]{2,1,0:T(8,128)(2,1)} %all_to_all.5) | data formatting | bytes 8388608 | tf_op jit(solution)/shard_map/reshape | solution.py:447
  364.0 1.3 fusion.3
  365.3 2.1 fusion.6
  (43 shorter events, 0.9 us)
Async XLA Ops:
  7.2 356.8 %reduce-scatter.2.cloned.1.call-start = ((), (), s32[]{:S(2)}) async-start(), calls=%async_computation.2 | async-start | bytes 9748480 | tf_op jit(solution)/shard_map/reduce_scatter | solution.py:463
  114.4 0.7 copy-start.8
  114.5 0.9 copy-start.7
  114.5 13.4 %copy-start.9 = (f32[2,256]{1,0:T(2,128)S(1)}, f32[2,256]{1,0:T(2,128)}, u32[]{:S(2)}) copy-start(f32[2,256]{1,0:T(2,128)} %param.15) | copy-start | bytes 6148
  129.0 3.6 copy-start.1
  142.2 4.6 %copy-start = (bf16[32,128,2,256]{3,2,1,0:T(2,128)(2,1)S(1)}, bf16[32,128,2,256]{3,2,1,0:T(2,128)(2,1)}, u32[]{:S(2)}) copy-start(bf16[32,128,2,256]{3,2,1,0:T(2,128)(2,1)} %param.17) | copy-start | bytes 12582916
  172.5 18.5 %copy-start.2 = (bf16[16,320,256]{2,1,0:T(8,128)(2,1)S(1)}, bf16[16,320,256]{2,1,0:T(8,128)(2,1)}, u32[]{:S(2)}) copy-start(bf16[16,320,256]{2,1,0:T(8,128)(2,1)} %get-tuple-element.8) | copy-start | bytes 7864324
  198.1 0.7 copy-start.10
  198.1 1.0 copy-start.4
  198.1 1.2 copy-start.5
  357.0 8.2 %copy-start.3 = (bf16[56,5120]{1,0:T(8,128)(2,1)S(1)}, bf16[56,5120]{1,0:T(8,128)(2,1)}, u32[]{:S(2)}) copy-start(bf16[56,5120]{1,0:T(8,128)(2,1)} %tok_ref.1) | copy-start | bytes 1720324
  357.0 8.2 %copy-start.6 = (f32[5120]{0:T(1024)S(1)}, f32[5120]{0:T(1024)}, u32[]{:S(2)}) copy-start(f32[5120]{0:T(1024)} %param.16) | copy-start | bytes 61444
Sparse Core Ops, SparseCore 0:
  198.3 146.9 reduce-scatter.1
where the time goes:
time: 375 us; the launch traced here: 374 us
  blocking collectives  153 us (41%)
  Pallas kernels  119 us (32%)
  local copies, waits for them, and re-layouts  43.8 us (12%)
  matrix products  24 us (6%)
  other arithmetic  20.1 us (5%)
  between operations  14.3 us (4%)
    all_to_all x1, blocking collectives, body(): lax.all_to_all(outgoing.reshape(n_req, page_span, 2 * local_width), 'req'...  153 us
    pallas_call x1, Pallas kernels, gather_all(): pl.pallas_call(functools.partial(gather_kernel, n_tp // 2, n_req // 4), o...  91.4 us
    pallas_call x1, Pallas kernels, attend(): pl.pallas_call(attend_kernel, out_shape=jax.ShapeDtypeStruct(q.shape, jnp...  18.5 us
    dot_general x1, matrix products, body(): jnp.dot(block_tokens, qkv_full, preferred_element_type=jnp.float32)  12.1 us
    unnamed x31, local copies, waits for them, and re-layouts  12 us
    pallas_call x1, Pallas kernels, sum_over_tp(): pl.pallas_call(functools.partial(sum_kernel, count), out_shape=jax.ShapeD...  9.13 us
  transfers between devices with their start and end apart: 1, of which 0 were waited for; matrix products, arithmetic and copies ran while one was open for 3% of the time, Pallas kernels for 0%

commit v1 on v0

--- a/solution.py
+++ b/solution.py
@@ -92,7 +92,7 @@
 
 
 def attend_kernel(
-    bounds_ref, q_ref, kn_ref, vn_ref, kt_ref, vp_ref, row_ref, col_ref, key_ref, o_ref
+    bounds_ref, order_ref, q_ref, kn_ref, vn_ref, kp_ref, vp_ref, row_ref, col_ref, key_ref, o_ref
 ):
     block_len, width = q_ref.shape
     heads_here = width // HEAD
@@ -128,13 +128,18 @@
         def step(j, carry):
             off = pl.multiple_of(j * CHUNK, CHUNK)
             mask = row_req == key_ref[:, pl.ds(off, CHUNK)]
+            pages = [
+                pl.ds(pl.multiple_of(order_ref[0, j * (CHUNK // PAGE) + e] * PAGE, PAGE), PAGE)
+                for e in range(CHUNK // PAGE)
+            ]
             out = []
             for h in range(heads_here):
                 cols = slice(h * HEAD, (h + 1) * HEAD)
                 top, total, mixed = carry[3 * h : 3 * h + 3]
-                scores = jnp.dot(
+                scores = lax.dot_general(
                     q_ref[tile_rows, cols],
-                    kt_ref[cols, pl.ds(off, CHUNK)],
+                    jnp.concatenate([kp_ref[page, cols] for page in pages], axis=0),
+                    (((1,), (1,)), ((), ())),
                     preferred_element_type=jnp.float32,
                 )
                 scores = jnp.where(mask, scores * scale, masked_score)
@@ -144,7 +149,7 @@
                 total = total * fade + jnp.sum(weights, axis=1, keepdims=True)
                 mixed = mixed * fade + jnp.dot(
                     weights.astype(jnp.bfloat16),
-                    vp_ref[pl.ds(off, CHUNK), cols],
+                    jnp.concatenate([vp_ref[page, cols] for page in pages], axis=0),
                     preferred_element_type=jnp.float32,
                 )
                 out += [new_top, total, mixed]
@@ -159,18 +164,18 @@
     lax.fori_loop(0, block_len // QTILE, tile, 0)
 
 
-def attend(bounds, q, kn, vn, kt, vp, row_req, col_req, key_req):
+def attend(bounds, order, q, kn, vn, kp, vp, row_req, col_req, key_req):
     vmem = pl.BlockSpec(memory_space=pltpu.VMEM)
     return pl.pallas_call(
         attend_kernel,
         out_shape=jax.ShapeDtypeStruct(q.shape, jnp.bfloat16),
-        in_specs=[pl.BlockSpec(memory_space=pltpu.SMEM)] + [vmem] * 8,
+        in_specs=[pl.BlockSpec(memory_space=pltpu.SMEM)] * 2 + [vmem] * 8,
         out_specs=vmem,
         cost_estimate=pl.CostEstimate(
             flops=4000000000, bytes_accessed=40000000, transcendentals=4000000
         ),
         name="paged_attention",
-    )(bounds, q, kn, vn, kt, vp, row_req, col_req, key_req)
+    )(bounds, order, q, kn, vn, kp, vp, row_req, col_req, key_req)
 
 
 def gather_kernel(
@@ -375,7 +380,6 @@
 
     lengths_row = lengths[0]
     prefix_row = prefix_pages[0]
-    order_row = pool_order[0]
     request_of, positions, starts_at = token_layout(lengths_row, prefix_row, block_len)
     half_dim = HEAD // 2
     frequency = rope_base ** (-(2.0 * jnp.arange(half_dim, dtype=jnp.float32)) / HEAD)
@@ -389,10 +393,8 @@
     page_ids = jnp.arange(pool_count, dtype=jnp.int32)
     page_request = jnp.sum((page_ids[:, None] >= page_ends[None, :]).astype(jnp.int32), axis=1)
     key_req = jnp.repeat(page_request, PAGE)[None, :]
-    pool_keys = jnp.take(pool_cache[:, :, 0, :], order_row, axis=0)
-    pool_values = jnp.take(pool_cache[:, :, 1, :], order_row, axis=0)
-    keys_t = pool_keys.reshape(pool_count * PAGE, local_width).T
-    pool_values = pool_values.reshape(pool_count * PAGE, local_width)
+    pool_keys = pool_cache[:, :, 0, :].reshape(pool_count * PAGE, local_width)
+    pool_values = pool_cache[:, :, 1, :].reshape(pool_count * PAGE, local_width)
     tiles = block_len // QTILE
     first_req = request_of.reshape(tiles, QTILE)[:, 0]
     last_req = request_of.reshape(tiles, QTILE)[:, -1]
@@ -426,37 +428,58 @@
     value_new = values_raw.astype(jnp.bfloat16)
 
     page_span = CAP * PAGE
-    owner_pick = (owners[0][None, :] == jnp.arange(n_req, dtype=jnp.int32)[:, None]).astype(jnp.int32)
-    start_of = jnp.sum(owner_pick * starts_at[None, :], axis=1)
-    length_of = jnp.sum(owner_pick * lengths_row[None, :], axis=1)
+    half = n_req // 2
+    my_half = lax.axis_index("req") // half
+    across = [(r, (r + half) % n_req) for r in range(n_req)]
+    kv_new = jnp.concatenate([key_rot, value_new], axis=1)
+    kv_new, query_rot = lax.optimization_barrier((kv_new, query_rot))
+    kv_far = lax.ppermute(kv_new, "req", across)
+    table = jnp.stack([starts_at, lengths_row, owners[0]])
+    table_far = lax.ppermute(table, "req", across)
+    attention = attend(
+        bounds,
+        pool_order,
+        query_rot,
+        key_rot,
+        value_new,
+        pool_keys,
+        pool_values,
+        request_of[:, None],
+        request_of[None, :],
+        key_req,
+    )
+    attention, kv_far, table_far = lax.optimization_barrier((attention, kv_far, table_far))
     offsets = jnp.arange(page_span, dtype=jnp.int32)
-    source = jnp.where(
-        offsets[None, :] < length_of[:, None], start_of[:, None] + offsets[None, :], -1
-    ).reshape(-1)
     token_ids = jnp.arange(block_len, dtype=jnp.int32)
-    select = (source[:, None] == token_ids[None, :]).astype(jnp.bfloat16)
-    kv_new = jnp.concatenate([key_rot, value_new], axis=1)
-    outgoing = jnp.dot(select, kv_new, preferred_element_type=jnp.float32).astype(jnp.bfloat16)
+    here = my_half * half + jnp.arange(half, dtype=jnp.int32)
+
+    def take_rows(rows, starts, sizes, owner_row):
+        owner_pick = (owner_row[None, :] == here[:, None]).astype(jnp.int32)
+        start_of = jnp.sum(owner_pick * starts[None, :], axis=1)
+        length_of = jnp.sum(owner_pick * sizes[None, :], axis=1)
+        source = jnp.where(
+            offsets[None, :] < length_of[:, None], start_of[:, None] + offsets[None, :], -1
+        ).reshape(-1)
+        select = (source[:, None] == token_ids[None, :]).astype(jnp.bfloat16)
+        taken = jnp.dot(select, rows, preferred_element_type=jnp.float32).astype(jnp.bfloat16)
+        return taken.reshape(half, page_span, 2 * local_width)
+
+    near = take_rows(kv_new, table[0], table[1], table[2])
+    remote = take_rows(kv_far, table_far[0], table_far[1], table_far[2])
+    outgoing = jnp.stack(
+        [jnp.where(my_half == 0, near, remote), jnp.where(my_half == 0, remote, near)], axis=1
+    )
     arrived = lax.all_to_all(
-        outgoing.reshape(n_req, page_span, 2 * local_width),
+        outgoing,
         "req",
         split_axis=0,
         concat_axis=0,
         tiled=True,
-    )
+        axis_index_groups=[list(range(half)), list(range(half, n_req))],
+    )
+    arrived = jnp.swapaxes(arrived, 0, 1)
     handed_pages = arrived.reshape(n_req * CAP, PAGE, 2, local_width)
 
-    attention = attend(
-        bounds,
-        query_rot,
-        key_rot,
-        value_new,
-        keys_t,
-        pool_values,
-        request_of[:, None],
-        request_of[None, :],
-        key_req,
-    )
     partial = lax.dot_general(
         attention, out_full, (((1,), (1,)), ((), ())), preferred_element_type=jnp.float32
     ).astype(jnp.bfloat16)

time: 375 us -> 310 us (0.83)
  blocking collectives: 153 us -> 55.7 us
  waiting for transfers between devices: 0.02 us -> 35.8 us
  local copies, waits for them, and re-layouts: 43.8 us -> 36 us
    all_to_all x1, blocking collectives: 153 us -> 55.7 us  [body(): lax.all_to_all(outgoing, 'req', split_axis=0, concat_axis=0, tiled=True,...]
    reduce_scatter x1, waiting for transfers between devices: 0.01 us -> 35.8 us  [body(): lax.psum_scatter(partial, 'tp', scatter_dimension=0, tiled=True)]
    reshape x3 -> x1, local copies, waits for them, and re-layouts: 11.1 us -> 0.08 us  [the longest x1 6.95 us: body(): handed_pages = arrived.reshape(n_req * CAP, PAGE, 2, local_width)]
    unnamed x31 -> x40, local copies, waits for them, and re-layouts: 12 us -> 20.7 us
    gather x2 -> x0, local copies, waits for them, and re-layouts: 5.84 us -> none  [the longest x1 3.57 us: body(): pool_values = jnp.take(pool_cache[:, :, 1, :], order_row, axis=0)]
    select_n x2 -> x0, other arithmetic: 4.67 us -> none  [the longest x1 4.01 us: body(): pool_values = jnp.take(pool_cache[:, :, 1, :], order_row, axis=0)]
  transfers between devices with their start and end apart: 1 -> 3, of which waited for: 0 -> 1; matrix products, arithmetic and copies ran while one was open for 3% -> 11% of each run, Pallas kernels for 0% -> 7%
where the time goes in v1:
time: 310 us
  Pallas kernels  122 us (39%)
  blocking collectives  55.7 us (18%)
  local copies, waits for them, and re-layouts  36 us (12%)
  waiting for transfers between devices  35.8 us (12%)
  matrix products  25.7 us (8%)
  other arithmetic  16.8 us (5%)
  between operations  14.4 us (5%)
    pallas_call x1, Pallas kernels, gather_all(): pl.pallas_call(functools.partial(gather_kernel, n_tp // 2, n_req // 4), o...  91.4 us
    all_to_all x1, blocking collectives, body(): lax.all_to_all(outgoing, 'req', split_axis=0, concat_axis=0, tiled=True,...  55.7 us
    reduce_scatter x1, waiting for transfers between devices, body(): lax.psum_scatter(partial, 'tp', scatter_dimension=0, tiled=True)  35.8 us
    pallas_call x1, Pallas kernels, attend(): pl.pallas_call(attend_kernel, out_shape=jax.ShapeDtypeStruct(q.shape, jnp...  21.6 us
    unnamed x40, local copies, waits for them, and re-layouts  20.7 us
    dot_general x1, matrix products, body(): jnp.dot(block_tokens, qkv_full, preferred_element_type=jnp.float32)  12.1 us
    slice x1, local copies, waits for them, and re-layouts, body(): pool_values = pool_cache[:, :, 1, :].reshape(pool_count * PAGE, local_width)  9.22 us
    pallas_call x1, Pallas kernels, sum_over_tp(): pl.pallas_call(functools.partial(sum_kernel, count), out_shape=jax.ShapeD...  9.14 us
  transfers between devices with their start and end apart: 3, of which 1 were waited for; matrix products, arithmetic and copies ran while one was open for 11% of the time, Pallas kernels for 7%

profile of v1, /device:TPU:1, one launch (start us, length us, event | category | flops | bytes accessed | tf_op | source)
XLA Modules:
  0.0 309.8 jit_solution(8230908746255513476)
XLA Ops:
  7.2 1.3 copy.76
  8.6 1.0 copy.77.wq_ref
  9.6 91.4 %gather_all.1 = (bf16[16,56,5120]{2,1,0:T(8,128)(2,1)}, bf16[16,320,768]{2,1,0:T(8,128)(2,1)}, bf16[16,320,256]{2,1,0:T(8,128)(2,1)}) custom-call(bf16[56,5120]{1,0:T(8,128)(2,1)} %tok_ref.1, bf16[320,768]{1,0:T(8,128)(2,1)} %copy.77.wq_ref, bf16[320,256]{1,0:T(8,128)(2,1)} %bitcast.94), custom_call_target="tpu_custom_call" | custom-call | tf_op jit(solution)/shard_map/gather_all/pallas_call | solution.py:336
  101.0 12.1 %fusion.19 = f32[896,768]{0,1:T(8,128)S(1)} fusion(bf16[896,5120]{1,0:T(8,128)(2,1)} %bitcast.106, bf16[5120,768]{1,0:T(8,128)(2,1)} %bitcast.107), kind=kOutput, calls=%fused_computation.88 | convolution fusion | flops 7046430720 | bytes 19791872 | tf_op jit(solution)/shard_map/dot_general | solution.py:407
  113.1 0.1 multiply_reduce_fusion.1
  113.3 0.6 pad_maximum_fusion.4.x_ref
  113.9 0.8 slice.78
  114.7 9.1 %sum_squares.1 = f32[2,896]{1,0:T(2,128)} custom-call(f32[2,896]{1,0:T(2,128)} %pad_maximum_fusion.4.x_ref), custom_call_target="tpu_custom_call" | custom-call | flops 100000 | bytes 20000000 | tf_op jit(solution)/shard_map/sum_squares/pallas_call | solution.py:78
  123.9 0.7 add_rsqrt_fusion
  124.6 1.1 multiply_multiply_fusion
  125.8 0.9 copy.92
  126.8 0.9 copy.93
  127.8 0.8 fusion.16
  128.6 1.8 copy.94
  130.4 1.3 copy.95
  131.8 0.1 reduce.2
  132.2 0.6 subtract_bitcast_fusion
  132.9 1.7 multiply_cosine_fusion
  134.6 3.2 %subtract_convert_fusion = (bf16[896,2,64]{2,1,0:T(2,128)(2,1)S(1)}, bf16[896,2,64]{2,1,0:T(2,128)(2,1)S(1)}, bf16[896,2,64]{2,1,0:T(2,128)(2,1)S(1)}, bf16[896,2,64]{2,1,0:T(2,128)(2,1)S(1)}) fusion(f32[896,2,64]{2,1,0:T(2,128)} %copy.95, f32[896,2,64]{2,1,0:T(2,128)S(1)} %copy.94, f32[896,64]{1,0:T(8,128)S(1)} %get-tuple-element.53, ...), kind=kLoop, calls=%fused_computation.20 | loop fusion | flops 1835008 | bytes 3211264 | tf_op jit(solution)/shard_map/convert
  137.8 2.5 pad_maximum_fusion.2
  140.4 0.2 copy.98.vn_ref
  140.6 0.9 copy.105
  141.6 2.7 collective-permute-start
  144.3 0.6 pad_add_fusion
  144.9 0.4 collective-permute-start.1
  145.3 1.0 broadcast_in_dim.74.row_ref
  146.2 0.6 broadcast_in_dim.39.col_ref
  146.8 0.2 slice_reduce_fusion.1
  147.0 0.2 select_reduce_fusion.2
  147.2 9.2 %fusion.15 = (bf16[32,128,1,256]{3,2,1,0:T(2,128)(2,1)S(1)}, bf16[32,128,1,256]{3,2,1,0:T(2,128)(2,1)S(1)}) fusion(bf16[32,128,2,256]{3,2,1,0:T(2,128)(2,1)} %param.15), kind=kLoop, calls=%fused_computation.84 | loop fusion | bytes 8388608 | tf_op jit(solution)/shard_map/slice | solution.py:397
  156.5 1.8 copy.96
  158.3 1.9 copy.97
  160.1 0.2 select_reduce_fusion.1
  160.3 0.6 pad_add_fusion.1.bounds_ref
  161.0 0.7 broadcast_in_dim.40
  161.6 21.6 %paged_attention.1 = bf16[896,256]{1,0:T(8,128)(2,1)} custom-call(s32[2,7]{1,0:T(2,128)} %pad_add_fusion.1.bounds_ref, s32[1,32]{1,0:T(1,128)} %order_ref.1, bf16[896,256]{1,0:T(8,128)(2,1)} %bitcast.93, bf16[896,256]{1,0:T(8,128)(2,1)} %bitcast.90, bf16[896,256]{1,0:T(8,128)(2,1)} %copy-done.4, bf16[4096,256]{1,0:T(8,128)(2,1)} %bitcast.85, ...), custom_call_target="tpu_custom_call" | custom-call | flops 4000000000 | bytes 40000000 | tf_op jit(solution)/shard_map/paged_attention/pallas_call | solution.py:169
  183.3 7.1 %convolution_convert_fusion = bf16[896,5120]{1,0:T(8,128)(2,1)} fusion(bf16[896,256]{1,0:T(8,128)(2,1)} %paged_attention.1, bf16[5120,256]{1,0:T(8,128)(2,1)S(1)} %bitcast.83), kind=kOutput, calls=%fused_computation | convolution fusion | flops 2353397760 | bytes 12255232 | tf_op jit(solution)/shard_map/dot_general | solution.py:483
  190.5 0.8 slice_bitcast_fusion.1
  191.3 0.2 fusion.10
  191.6 2.6 fusion.5
  194.3 3.8 %broadcast_select_fusion.1 = (bf16[2048,512]{1,0:T(8,128)(2,1)S(1)}, bf16[2048,512]{1,0:T(8,128)(2,1)S(1)}) fusion(bf16[2048,512]{1,0:T(8,128)(2,1)S(1)} %fusion.5, pred[]{:T(512)S(6)} %eq.112, bf16[896,512]{1,0:T(8,128)(2,1)} %collective-permute-done, s32[2048]{0:T(1024)S(1)} %bitcast.97), kind=kOutput, calls=%fused_computation.11 | convolution fusion | flops 1884028928 | bytes 7217153 | tf_op jit(solution)/shard_map/dot_general | solution.py:464
  198.1 0.4 pad_maximum_fusion
  198.5 55.7 %all_to_all.5 = bf16[8,2,256,512]{3,2,1,0:T(8,128)(2,1)S(1)} all-to-all(bf16[8,2,256,512]{3,2,1,0:T(8,128)(2,1)S(1)} %pad_maximum_fusion), channel_id=1, replica_groups={{0,16,32,48,64,80,96,112},{128,144,160,176,192,208,224,240},{1,17,33,49..., dimensions={0} | all-to-all | bytes 8388608 | tf_op jit(solution)/shard_map/all_to_all | solution.py:472
  254.2 2.5 copy.90
  256.7 7.0 %reshape.354 = bf16[32,128,2,256]{3,2,1,0:T(2,128)(2,1)} reshape(bf16[2,8,256,512]{3,2,1,0:T(8,128)(2,1)} %copy.90) | data formatting | bytes 8388608
  263.6 35.8 %reduce-scatter.2.cloned.1.call-done = bf16[56,5120]{1,0:T(8,128)(2,1)} async-done(((bf16[896,5120]{1,0:T(8,128)(2,1)}), bf16[56,5120]{1,0:T(8,128)(2,1)}) %reduce-scatter.2.cloned.1.call-update) | async-done | bytes 573456 | tf_op jit(solution)/shard_map/reduce_scatter | solution.py:486
  299.5 1.3 fusion.6
  300.8 2.1 fusion.9
  (55 shorter events, 1.2 us)
Async XLA Ops:
  7.2 292.3 %reduce-scatter.2.cloned.1.call-start = ((), (), s32[]{:S(2)}) async-start(), calls=%async_computation.2 | async-start | bytes 9748480 | tf_op jit(solution)/shard_map/reduce_scatter | solution.py:486
  113.1 11.5 %copy-start.9 = (f32[2,256]{1,0:T(2,128)S(1)}, f32[2,256]{1,0:T(2,128)}, u32[]{:S(2)}) copy-start(f32[2,256]{1,0:T(2,128)} %param.13) | copy-start | bytes 6148
  125.8 2.0 copy-start
  126.8 4.9 %copy-start.8 = (s32[1,16]{1,0:T(1,128)S(1)}, s32[1,16]{1,0:T(1,128)}, u32[]{:S(2)}) copy-start(s32[1,16]{1,0:T(1,128)} %param.17) | copy-start | bytes 196
  126.8 5.1 %copy-start.7 = (s32[1,16]{1,0:T(1,128)S(1)}, s32[1,16]{1,0:T(1,128)}, u32[]{:S(2)}) copy-start(s32[1,16]{1,0:T(1,128)} %param.16) | copy-start | bytes 196
  137.8 2.6 copy-start.5
  140.3 4.0 %copy-start.10 = (s32[1,16]{1,0:T(1,128)S(1)}, s32[1,16]{1,0:T(1,128)}, u32[]{:S(2)}) copy-start(s32[1,16]{1,0:T(1,128)} %param.19) | copy-start | bytes 196
  140.3 6.7 %copy-start.12 = (s32[16]{0:T(128)S(1)}, s32[16]{0:T(128)}, u32[]{:S(2)}) copy-start(s32[16]{0:T(128)} %get-tuple-element.59) | copy-start | bytes 196
  140.4 16.1 %copy-start.3 = (bf16[112,8,2,128]{3,1,2,0:T(8,128)(2,1)}, bf16[112,8,2,128]{3,1,2,0:T(8,128)(2,1)S(1)}, u32[]{:S(2)}) copy-start(bf16[112,8,2,128]{3,1,2,0:T(8,128)(2,1)S(1)} %copy.106) | copy-start | bytes 1376260
  140.6 15.8 %copy-start.4 = (bf16[896,256]{1,0:T(8,128)(2,1)}, bf16[896,256]{1,0:T(8,128)(2,1)S(1)}, u32[]{:S(2)}) copy-start(bf16[896,256]{1,0:T(8,128)(2,1)S(1)} %copy.98.vn_ref) | copy-start | bytes 1376260
  141.6 41.7 %collective-permute-start = (bf16[896,512]{1,0:T(8,128)(2,1)S(1)}, bf16[896,512]{1,0:T(8,128)(2,1)}, u32[]{:S(2)}, u32[]{:S(2)}) collective-permute-start(bf16[896,512]{1,0:T(8,128)(2,1)S(1)} %pad_maximum_fusion.1), channel_id=1, source_target_pairs={{0,128},{16,144},{32,160},{48,176},{64,192},{80,208},{96,224},{112... | collective-permute-start | bytes 2752520 | tf_op jit(solution)/shard_map/ppermute | solution.py:436
  144.9 38.4 %collective-permute-start.1 = (s32[3,16]{1,0:T(4,128)}, s32[3,16]{1,0:T(4,128)}, u32[]{:S(2)}, u32[]{:S(2)}) collective-permute-start(s32[3,16]{1,0:T(4,128)} %pad_add_fusion), channel_id=1, source_target_pairs={{0,128},{16,144},{32,160},{48,176},{64,192},{80,208},{96,224},{112... | collective-permute-start | bytes 584 | tf_op jit(solution)/shard_map/ppermute | solution.py:438
  161.6 21.6 %copy-start.1 = (bf16[16,320,256]{2,1,0:T(8,128)(2,1)S(1)}, bf16[16,320,256]{2,1,0:T(8,128)(2,1)}, u32[]{:S(2)}) copy-start(bf16[16,320,256]{2,1,0:T(8,128)(2,1)} %get-tuple-element.15) | copy-start | bytes 7864324
  190.4 0.9 copy-start.11
  256.6 44.1 %copy-start.2 = (bf16[56,5120]{1,0:T(8,128)(2,1)S(1)}, bf16[56,5120]{1,0:T(8,128)(2,1)}, u32[]{:S(2)}) copy-start(bf16[56,5120]{1,0:T(8,128)(2,1)} %tok_ref.1) | copy-start | bytes 1720324
  256.6 44.1 %copy-start.6 = (f32[5120]{0:T(1024)S(1)}, f32[5120]{0:T(1024)}, u32[]{:S(2)}) copy-start(f32[5120]{0:T(1024)} %param.14) | copy-start | bytes 61444
Sparse Core Ops, SparseCore 0:
  190.6 108.8 reduce-scatter.1

commit v2 on v1

--- a/solution.py
+++ b/solution.py
@@ -92,7 +92,7 @@
 
 
 def attend_kernel(
-    bounds_ref, order_ref, q_ref, kn_ref, vn_ref, kp_ref, vp_ref, row_ref, col_ref, key_ref, o_ref
+    bounds_ref, order_ref, q_ref, kn_ref, vn_ref, pool_ref, row_ref, col_ref, key_ref, o_ref
 ):
     block_len, width = q_ref.shape
     heads_here = width // HEAD
@@ -135,10 +135,11 @@
             out = []
             for h in range(heads_here):
                 cols = slice(h * HEAD, (h + 1) * HEAD)
+                value_cols = slice(width + h * HEAD, width + (h + 1) * HEAD)
                 top, total, mixed = carry[3 * h : 3 * h + 3]
                 scores = lax.dot_general(
                     q_ref[tile_rows, cols],
-                    jnp.concatenate([kp_ref[page, cols] for page in pages], axis=0),
+                    jnp.concatenate([pool_ref[page, cols] for page in pages], axis=0),
                     (((1,), (1,)), ((), ())),
                     preferred_element_type=jnp.float32,
                 )
@@ -149,7 +150,7 @@
                 total = total * fade + jnp.sum(weights, axis=1, keepdims=True)
                 mixed = mixed * fade + jnp.dot(
                     weights.astype(jnp.bfloat16),
-                    jnp.concatenate([vp_ref[page, cols] for page in pages], axis=0),
+                    jnp.concatenate([pool_ref[page, value_cols] for page in pages], axis=0),
                     preferred_element_type=jnp.float32,
                 )
                 out += [new_top, total, mixed]
@@ -164,18 +165,18 @@
     lax.fori_loop(0, block_len // QTILE, tile, 0)
 
 
-def attend(bounds, order, q, kn, vn, kp, vp, row_req, col_req, key_req):
+def attend(bounds, order, q, kn, vn, pool, row_req, col_req, key_req):
     vmem = pl.BlockSpec(memory_space=pltpu.VMEM)
     return pl.pallas_call(
         attend_kernel,
         out_shape=jax.ShapeDtypeStruct(q.shape, jnp.bfloat16),
-        in_specs=[pl.BlockSpec(memory_space=pltpu.SMEM)] * 2 + [vmem] * 8,
+        in_specs=[pl.BlockSpec(memory_space=pltpu.SMEM)] * 2 + [vmem] * 7,
         out_specs=vmem,
         cost_estimate=pl.CostEstimate(
             flops=4000000000, bytes_accessed=40000000, transcendentals=4000000
         ),
         name="paged_attention",
-    )(bounds, order, q, kn, vn, kp, vp, row_req, col_req, key_req)
+    )(bounds, order, q, kn, vn, pool, row_req, col_req, key_req)
 
 
 def gather_kernel(
@@ -393,8 +394,7 @@
     page_ids = jnp.arange(pool_count, dtype=jnp.int32)
     page_request = jnp.sum((page_ids[:, None] >= page_ends[None, :]).astype(jnp.int32), axis=1)
     key_req = jnp.repeat(page_request, PAGE)[None, :]
-    pool_keys = pool_cache[:, :, 0, :].reshape(pool_count * PAGE, local_width)
-    pool_values = pool_cache[:, :, 1, :].reshape(pool_count * PAGE, local_width)
+    pool_rows = pool_cache.reshape(pool_count * PAGE, 2 * local_width)
     tiles = block_len // QTILE
     first_req = request_of.reshape(tiles, QTILE)[:, 0]
     last_req = request_of.reshape(tiles, QTILE)[:, -1]
@@ -442,8 +442,7 @@
         query_rot,
         key_rot,
         value_new,
-        pool_keys,
-        pool_values,
+        pool_rows,
         request_of[:, None],
         request_of[None, :],
         key_req,

time: 310 us -> 304 us (0.981)
  local copies, waits for them, and re-layouts: 36 us -> 28.1 us
  blocking collectives: 55.7 us -> 62.6 us
    slice x1 -> x0, local copies, waits for them, and re-layouts: 9.22 us -> none  [body(): pool_values = pool_cache[:, :, 1, :].reshape(pool_count * PAGE, local_width)]
    all_to_all x1, blocking collectives: 55.7 us -> 62.6 us  [body(): lax.all_to_all(outgoing, 'req', split_axis=0, concat_axis=0, tiled=True,...]
    unnamed x40 -> x39, local copies, waits for them, and re-layouts: 20.7 us -> 22 us
  transfers between devices with their start and end apart: 3 -> 3, of which waited for: 1 -> 1; matrix products, arithmetic and copies ran while one was open for 11% -> 9% of each run, Pallas kernels for 7% -> 6%
where the time goes in v2:
time: 304 us; the launch traced here: 305 us
  Pallas kernels  119 us (39%)
  blocking collectives  62.6 us (21%)
  waiting for transfers between devices  35.4 us (12%)
  local copies, waits for them, and re-layouts  28.1 us (9%)
  matrix products  25.7 us (8%)
  other arithmetic  16.8 us (6%)
  between operations  14.4 us (5%)
  starting transfers between devices  3.09 us (1%)
    pallas_call x1, Pallas kernels, gather_all(): pl.pallas_call(functools.partial(gather_kernel, n_tp // 2, n_req // 4), o...  91.4 us
    all_to_all x1, blocking collectives, body(): lax.all_to_all(outgoing, 'req', split_axis=0, concat_axis=0, tiled=True,...  62.6 us
    reduce_scatter x1, waiting for transfers between devices, body(): lax.psum_scatter(partial, 'tp', scatter_dimension=0, tiled=True)  35.4 us
    unnamed x39, local copies, waits for them, and re-layouts  22 us
    pallas_call x1, Pallas kernels, attend(): pl.pallas_call(attend_kernel, out_shape=jax.ShapeDtypeStruct(q.shape, jnp...  18.7 us
    dot_general x1, matrix products, body(): jnp.dot(block_tokens, qkv_full, preferred_element_type=jnp.float32)  12.1 us
    pallas_call x1, Pallas kernels, sum_over_tp(): pl.pallas_call(functools.partial(sum_kernel, count), out_shape=jax.ShapeD...  9.14 us
    dot_general x1, matrix products, body(): lax.dot_general(attention, out_full, (((1,), (1,)), ((), ())), preferred_...  7.12 us
  transfers between devices with their start and end apart: 3, of which 1 were waited for; matrix products, arithmetic and copies ran while one was open for 9% of the time, Pallas kernels for 6%

profile of v2, /device:TPU:1, one launch (start us, length us, event | category | flops | bytes accessed | tf_op | source)
XLA Modules:
  0.0 305.3 jit_solution(2890444347989035732)
XLA Ops:
  7.2 1.3 copy.68
  8.6 1.0 copy.69.wq_ref
  9.6 91.4 %gather_all.1 = (bf16[16,56,5120]{2,1,0:T(8,128)(2,1)}, bf16[16,320,768]{2,1,0:T(8,128)(2,1)}, bf16[16,320,256]{2,1,0:T(8,128)(2,1)}) custom-call(bf16[56,5120]{1,0:T(8,128)(2,1)} %tok_ref.1, bf16[320,768]{1,0:T(8,128)(2,1)} %copy.69.wq_ref, bf16[320,256]{1,0:T(8,128)(2,1)} %bitcast.95), custom_call_target="tpu_custom_call" | custom-call | tf_op jit(solution)/shard_map/gather_all/pallas_call | solution.py:337
  101.0 12.1 %fusion.18 = f32[896,768]{0,1:T(8,128)S(1)} fusion(bf16[896,5120]{1,0:T(8,128)(2,1)} %bitcast.107, bf16[5120,768]{1,0:T(8,128)(2,1)} %bitcast.108), kind=kOutput, calls=%fused_computation.87 | convolution fusion | flops 7046430720 | bytes 19791872 | tf_op jit(solution)/shard_map/dot_general | solution.py:407
  113.1 0.1 multiply_reduce_fusion.1
  113.3 0.6 pad_maximum_fusion.4.x_ref
  113.9 0.8 slice.70
  114.7 9.1 %sum_squares.1 = f32[2,896]{1,0:T(2,128)} custom-call(f32[2,896]{1,0:T(2,128)} %pad_maximum_fusion.4.x_ref), custom_call_target="tpu_custom_call" | custom-call | flops 100000 | bytes 20000000 | tf_op jit(solution)/shard_map/sum_squares/pallas_call | solution.py:78
  123.9 0.7 add_rsqrt_fusion
  124.6 1.1 multiply_multiply_fusion
  125.8 0.9 copy.82
  126.8 0.9 copy.83
  127.8 0.8 fusion.15
  128.6 1.8 copy.84
  130.4 1.3 copy.85
  131.8 0.1 reduce.2
  132.0 0.1 reduce
  132.2 0.6 subtract_bitcast_fusion
  132.9 1.7 multiply_cosine_fusion
  134.6 3.2 %subtract_convert_fusion = (bf16[896,2,64]{2,1,0:T(2,128)(2,1)S(1)}, bf16[896,2,64]{2,1,0:T(2,128)(2,1)S(1)}, bf16[896,2,64]{2,1,0:T(2,128)(2,1)S(1)}, bf16[896,2,64]{2,1,0:T(2,128)(2,1)S(1)}) fusion(f32[896,2,64]{2,1,0:T(2,128)} %copy.85, f32[896,2,64]{2,1,0:T(2,128)S(1)} %copy.84, f32[896,64]{1,0:T(8,128)S(1)} %get-tuple-element.51, ...), kind=kLoop, calls=%fused_computation.20 | loop fusion | flops 1835008 | bytes 3211264 | tf_op jit(solution)/shard_map/convert
  137.8 2.5 pad_maximum_fusion.2
  140.4 0.2 copy.86.vn_ref
  140.6 0.9 copy.94
  141.6 2.7 collective-permute-start
  144.3 0.6 pad_add_fusion
  144.9 0.4 collective-permute-start.1
  145.3 1.0 broadcast_in_dim.74.row_ref
  146.2 0.6 broadcast_in_dim.39.col_ref
  146.8 0.2 slice_reduce_fusion.1
  147.0 0.2 select_reduce_fusion.2
  147.2 4.9 %copy.89 = bf16[512,8,2,256]{3,1,2,0:T(8,128)(2,1)} copy(bf16[512,8,2,256]{3,2,1,0:T(2,128)(2,1)} %bitcast.82) | data formatting | bytes 8388608
  152.2 0.2 select_reduce_fusion.1
  152.3 0.6 pad_add_fusion.1.bounds_ref
  152.9 0.1 convert_reduce_fusion.1
  153.0 0.7 broadcast_in_dim.40
  153.7 18.7 %paged_attention.1 = bf16[896,256]{1,0:T(8,128)(2,1)} custom-call(s32[2,7]{1,0:T(2,128)} %pad_add_fusion.1.bounds_ref, s32[1,32]{1,0:T(1,128)} %order_ref.1, bf16[896,256]{1,0:T(8,128)(2,1)} %bitcast.94, bf16[896,256]{1,0:T(8,128)(2,1)} %bitcast.91, bf16[896,256]{1,0:T(8,128)(2,1)} %copy-done.4, bf16[4096,512]{1,0:T(8,128)(2,1)} %bitcast.83, ...), custom_call_target="tpu_custom_call" | custom-call | flops 4000000000 | bytes 40000000 | tf_op jit(solution)/shard_map/paged_attention/pallas_call | solution.py:170
  172.4 7.1 %convolution_convert_fusion = bf16[896,5120]{1,0:T(8,128)(2,1)} fusion(bf16[896,256]{1,0:T(8,128)(2,1)} %paged_attention.1, bf16[5120,256]{1,0:T(8,128)(2,1)S(1)} %bitcast.86), kind=kOutput, calls=%fused_computation | convolution fusion | flops 2353397760 | bytes 12255232 | tf_op jit(solution)/shard_map/dot_general | solution.py:482
  179.6 0.8 slice_bitcast_fusion.1
  180.4 0.2 fusion.10
  180.8 2.6 fusion.5
  183.4 3.8 %broadcast_select_fusion.1 = (bf16[2048,512]{1,0:T(8,128)(2,1)S(1)}, bf16[2048,512]{1,0:T(8,128)(2,1)S(1)}) fusion(bf16[2048,512]{1,0:T(8,128)(2,1)S(1)} %fusion.5, pred[]{:T(512)S(6)} %eq.112, bf16[896,512]{1,0:T(8,128)(2,1)} %collective-permute-done, s32[2048]{0:T(1024)S(1)} %bitcast.98), kind=kOutput, calls=%fused_computation.11 | convolution fusion | flops 1884028928 | bytes 7217153 | tf_op jit(solution)/shard_map/dot_general | solution.py:463
  187.2 0.4 pad_maximum_fusion
  187.6 62.6 %all_to_all.5 = bf16[8,2,256,512]{3,2,1,0:T(8,128)(2,1)S(1)} all-to-all(bf16[8,2,256,512]{3,2,1,0:T(8,128)(2,1)S(1)} %pad_maximum_fusion), channel_id=1, replica_groups={{0,16,32,48,64,80,96,112},{128,144,160,176,192,208,224,240},{1,17,33,49..., dimensions={0} | all-to-all | bytes 8388608 | tf_op jit(solution)/shard_map/all_to_all | solution.py:471
  250.2 2.5 copy.80
  252.7 7.0 %reshape.358 = bf16[32,128,2,256]{3,2,1,0:T(2,128)(2,1)} reshape(bf16[2,8,256,512]{3,2,1,0:T(8,128)(2,1)} %copy.80) | data formatting | bytes 8388608
  259.7 35.4 %reduce-scatter.2.cloned.1.call-done = bf16[56,5120]{1,0:T(8,128)(2,1)} async-done(((bf16[896,5120]{1,0:T(8,128)(2,1)}), bf16[56,5120]{1,0:T(8,128)(2,1)}) %reduce-scatter.2.cloned.1.call-update) | async-done | bytes 573456 | tf_op jit(solution)/shard_map/reduce_scatter | solution.py:485
  295.1 1.3 fusion.6
  296.4 2.1 fusion.9
  (53 shorter events, 1.0 us)
Async XLA Ops:
  7.2 287.9 %reduce-scatter.2.cloned.1.call-start = ((), (), s32[]{:S(2)}) async-start(), calls=%async_computation.2 | async-start | bytes 9748480 | tf_op jit(solution)/shard_map/reduce_scatter | solution.py:485
  113.1 11.5 %copy-start.9 = (f32[2,256]{1,0:T(2,128)S(1)}, f32[2,256]{1,0:T(2,128)}, u32[]{:S(2)}) copy-start(f32[2,256]{1,0:T(2,128)} %param.13) | copy-start | bytes 6148
  125.8 2.0 copy-start
  126.8 4.9 %copy-start.8 = (s32[1,16]{1,0:T(1,128)S(1)}, s32[1,16]{1,0:T(1,128)}, u32[]{:S(2)}) copy-start(s32[1,16]{1,0:T(1,128)} %param.17) | copy-start | bytes 196
  126.8 5.1 %copy-start.7 = (s32[1,16]{1,0:T(1,128)S(1)}, s32[1,16]{1,0:T(1,128)}, u32[]{:S(2)}) copy-start(s32[1,16]{1,0:T(1,128)} %param.16) | copy-start | bytes 196
  137.8 2.6 copy-start.5
  140.3 4.0 %copy-start.10 = (s32[1,16]{1,0:T(1,128)S(1)}, s32[1,16]{1,0:T(1,128)}, u32[]{:S(2)}) copy-start(s32[1,16]{1,0:T(1,128)} %param.19) | copy-start | bytes 196
  140.3 6.7 %copy-start.12 = (s32[16]{0:T(128)S(1)}, s32[16]{0:T(128)}, u32[]{:S(2)}) copy-start(s32[16]{0:T(128)} %get-tuple-element.57) | copy-start | bytes 196
  140.4 11.8 %copy-start.3 = (bf16[112,8,2,128]{3,1,2,0:T(8,128)(2,1)}, bf16[112,8,2,128]{3,1,2,0:T(8,128)(2,1)S(1)}, u32[]{:S(2)}) copy-start(bf16[112,8,2,128]{3,1,2,0:T(8,128)(2,1)S(1)} %copy.95) | copy-start | bytes 1376260
  140.6 11.5 %copy-start.4 = (bf16[896,256]{1,0:T(8,128)(2,1)}, bf16[896,256]{1,0:T(8,128)(2,1)S(1)}, u32[]{:S(2)}) copy-start(bf16[896,256]{1,0:T(8,128)(2,1)S(1)} %copy.86.vn_ref) | copy-start | bytes 1376260
  141.6 30.8 %collective-permute-start = (bf16[896,512]{1,0:T(8,128)(2,1)S(1)}, bf16[896,512]{1,0:T(8,128)(2,1)}, u32[]{:S(2)}, u32[]{:S(2)}) collective-permute-start(bf16[896,512]{1,0:T(8,128)(2,1)S(1)} %pad_maximum_fusion.1), channel_id=1, source_target_pairs={{0,128},{16,144},{32,160},{48,176},{64,192},{80,208},{96,224},{112... | collective-permute-start | bytes 2752520 | tf_op jit(solution)/shard_map/ppermute | solution.py:436
  144.9 27.5 %collective-permute-start.1 = (s32[3,16]{1,0:T(4,128)}, s32[3,16]{1,0:T(4,128)}, u32[]{:S(2)}, u32[]{:S(2)}) collective-permute-start(s32[3,16]{1,0:T(4,128)} %pad_add_fusion), channel_id=1, source_target_pairs={{0,128},{16,144},{32,160},{48,176},{64,192},{80,208},{96,224},{112... | collective-permute-start | bytes 584 | tf_op jit(solution)/shard_map/ppermute | solution.py:438
  153.7 18.7 %copy-start.1 = (bf16[16,320,256]{2,1,0:T(8,128)(2,1)S(1)}, bf16[16,320,256]{2,1,0:T(8,128)(2,1)}, u32[]{:S(2)}) copy-start(bf16[16,320,256]{2,1,0:T(8,128)(2,1)} %get-tuple-element.15) | copy-start | bytes 7864324
  179.5 0.9 copy-start.11
  252.7 43.7 %copy-start.2 = (bf16[56,5120]{1,0:T(8,128)(2,1)S(1)}, bf16[56,5120]{1,0:T(8,128)(2,1)}, u32[]{:S(2)}) copy-start(bf16[56,5120]{1,0:T(8,128)(2,1)} %tok_ref.1) | copy-start | bytes 1720324
  252.7 43.7 %copy-start.6 = (f32[5120]{0:T(1024)S(1)}, f32[5120]{0:T(1024)}, u32[]{:S(2)}) copy-start(f32[5120]{0:T(1024)} %param.14) | copy-start | bytes 61444
Sparse Core Ops, SparseCore 0:
  179.7 115.3 reduce-scatter.1
